TPU v7x, 32 devices: a whole 2x2x4 slice. The times are simulated.
32 devices in a mesh: batch: 8 (over z, y), grp: 4 (over x, core).
Axes of the slice: x: 2, y: 2, z: 4, core: 2. Of those that a mesh axis runs over, the one named last changes fastest.
Arguments:
- tokens: bfloat16 [8192, 768], P(('batch', 'grp')), may hold values from -6 to 6
- dest: int32 [8192, 1], P(('batch', 'grp')), may hold values from 0 to 7; in each aligned block of 256 rows (0 to 255, 256 to 511, ...) at most 64 rows name the same one
- seg_ids: int32 [32, 512], P(('batch', 'grp')), may hold values from 0 to 7, never falling along the last dimension, each value on 1 to 128 neighbouring positions
- cot_out: bfloat16 [8192, 768], P(('batch', 'grp')), may hold values from -6 to 6
- cot_align: bfloat16 [8192, 1024], P(('batch', 'grp')), may hold values from -6 to 6
- ln1_gain: bfloat16 [768], replicated, may hold values from 0.5 to 1.5
- ln1_bias: bfloat16 [768], replicated, may hold values from -1 to 1
- w_qkv: bfloat16 [768, 2304], replicated, may hold values from -0.21875 to 0.21875
- q_bias: bfloat16 [768], replicated, may hold values from -1 to 1
- v_bias: bfloat16 [768], replicated, may hold values from -1 to 1
- w_out: bfloat16 [768, 768], replicated, may hold values from -1.75 to 1.75
- out_bias: bfloat16 [768], replicated, may hold values from -1 to 1
- ln2_gain: bfloat16 [768], replicated, may hold values from 0.5 to 1.5
- ln2_bias: bfloat16 [768], replicated, may hold values from -1 to 1
- w_up: bfloat16 [768, 3072], replicated, may hold values from -0.21875 to 0.21875
- up_bias: bfloat16 [3072], replicated, may hold values from -1 to 1
- w_down: bfloat16 [3072, 768], replicated, may hold values from -0.109375 to 0.109375
- down_bias: bfloat16 [768], replicated, may hold values from -1 to 1
- ln3_gain: bfloat16 [768], replicated, may hold values from 0.5 to 1.5
- ln3_bias: bfloat16 [768], replicated, may hold values from -1 to 1
- w_align: bfloat16 [768, 1024], replicated, may hold values from -0.21875 to 0.21875
- align_bias: bfloat16 [1024], replicated, may hold values from -1 to 1
Outputs:
- out_tokens: bfloat16 [8192, 768], P(('batch', 'grp'))
- aligned_tokens: bfloat16 [8192, 1024], P(('batch', 'grp'))
- grad_tokens: bfloat16 [8192, 768], P(('batch', 'grp'))
- grad_ln1_gain: float32 [768], replicated
- grad_ln1_bias: float32 [768], replicated
- grad_w_qkv: float32 [768, 2304], P('batch', 'grp')
- grad_q_bias: float32 [768], replicated
- grad_v_bias: float32 [768], replicated
- grad_w_out: float32 [768, 768], P('batch', 'grp')
- grad_out_bias: float32 [768], replicated
- grad_ln2_gain: float32 [768], replicated
- grad_ln2_bias: float32 [768], replicated
- grad_w_up: float32 [768, 3072], P('batch', 'grp')
- grad_up_bias: float32 [3072], replicated
- grad_w_down: float32 [3072, 768], P('batch', 'grp')
- grad_down_bias: float32 [768], replicated
- grad_ln3_gain: float32 [768], replicated
- grad_ln3_bias: float32 [768], replicated
- grad_w_align: float32 [768, 1024], P('batch', 'grp')
- grad_align_bias: float32 [1024], replicated
Inputs may be any that keep to these rules, and one draw needn't show every extreme that they name: `dest`: within the 256 rows of one device no destination is named by more than 64 rows, a bound that some block reaches. `seg_ids`: along each device's 512 slots the clip numbers never fall; each clip takes 1 to 128 slots and some clip exactly 128.
All inputs are finite; a program needn't handle non-finite values.
Results may differ from a plain program's by a relative error of at most 0.012.
Values may be sent and summed in bfloat16 or wider, within the bound.
No kernel may reach another device: no remote copies, remote signals or barrier semaphores. Data moves between devices by JAX's collectives and lax.ppermute only.
A program may use at most 192 MiB of HBM per device.

v0:
```python
import jax
import jax.numpy as jnp
from jax import lax
from jax.sharding import PartitionSpec as P

H = 12
layer_eps = 1e-06
masked_value = -1e30


def normalize(values, gain_row, shift_row):
    average = jnp.mean(values, axis=-1, keepdims=True)
    centered = values - average
    variance = jnp.mean(centered * centered, axis=-1, keepdims=True)
    return centered * lax.rsqrt(variance + layer_eps) * gain_row + shift_row


def exact_gelu(values):
    return jax.nn.gelu(values, approximate=False)


def row_matmul(left_side, right_side):
    return jnp.dot(left_side, right_side, preferred_element_type=jnp.float32)


def left_transposed(left_side, right_side):
    return lax.dot_general(
        left_side, right_side, (((0,), (0,)), ((), ())), preferred_element_type=jnp.float32
    )


def right_transposed(left_side, right_side):
    return lax.dot_general(
        left_side, right_side, (((1,), (1,)), ((), ())), preferred_element_type=jnp.float32
    )


def column_sum(values):
    return jnp.sum(values.astype(jnp.float32), axis=0)


def tiled_blocks(matrix, row_parts, column_parts):
    rows_total, columns_total = matrix.shape
    shaped = matrix.reshape(
        row_parts, rows_total // row_parts, column_parts, columns_total // column_parts
    )
    shaped = jnp.transpose(shaped, (0, 2, 1, 3))
    return shaped.reshape(
        row_parts * column_parts, rows_total // row_parts, columns_total // column_parts
    )


def per_device(
    tokens,
    dest,
    seg_ids,
    cot_out,
    cot_align,
    ln1_gain,
    ln1_bias,
    w_qkv,
    q_bias,
    v_bias,
    w_out,
    out_bias,
    ln2_gain,
    ln2_bias,
    w_up,
    up_bias,
    w_down,
    down_bias,
    ln3_gain,
    ln3_bias,
    w_align,
    align_bias,
):
    model_width = tokens.shape[1]
    align_width = cot_align.shape[1]
    seq_rows = seg_ids.shape[1]
    peer_count = lax.axis_size("batch")
    group_count = lax.axis_size("grp")
    capacity = seq_rows // peer_count
    head_count = H
    head_size = model_width // head_count
    score_scale = head_size ** (-0.5)
    targets = dest[:, 0]
    onehot = (targets[:, None] == jnp.arange(peer_count, dtype=jnp.int32)[None, :]).astype(
        jnp.int32
    )
    earlier = jnp.cumsum(onehot, axis=0) - onehot
    offset = jnp.sum(earlier * onehot, axis=1)
    slot_index = targets * capacity + offset

    def pack_rows(rows):
        empty = jnp.zeros((seq_rows,) + rows.shape[1:], rows.dtype)
        return empty.at[slot_index].set(rows).reshape((peer_count, capacity) + rows.shape[1:])

    flag_rows = jnp.ones((tokens.shape[0],), jnp.bfloat16)
    recv_rows, recv_grad, recv_align, recv_flag = (
        lax.all_to_all(pack_rows(tokens), "batch", split_axis=0, concat_axis=0, tiled=True),
        lax.all_to_all(pack_rows(cot_out), "batch", split_axis=0, concat_axis=0, tiled=True),
        lax.all_to_all(pack_rows(cot_align), "batch", split_axis=0, concat_axis=0, tiled=True),
        lax.all_to_all(pack_rows(flag_rows), "batch", split_axis=0, concat_axis=0, tiled=True),
    )
    inputs = recv_rows.reshape(seq_rows, model_width).astype(jnp.float32)
    is_live = recv_flag.reshape(seq_rows) > 0.5
    segments = seg_ids[0]
    key_index = jnp.arange(seq_rows, dtype=jnp.int32)
    block_rows = min(512, seq_rows)
    gain_one = ln1_gain.astype(jnp.float32)
    normed_one, norm_one_back = jax.vjp(normalize, inputs, gain_one, ln1_bias.astype(jnp.float32))
    act_one = normed_one.astype(jnp.bfloat16)
    joined = row_matmul(act_one, w_qkv)
    queries = (
        (joined[:, :model_width] + q_bias.astype(jnp.float32))
        .astype(jnp.bfloat16)
        .reshape(seq_rows, head_count, head_size)
    )
    key_rows = (
        joined[:, model_width : 2 * model_width]
        .astype(jnp.bfloat16)
        .reshape(seq_rows, head_count, head_size)
    )
    value_rows = (
        (joined[:, 2 * model_width :] + v_bias.astype(jnp.float32))
        .astype(jnp.bfloat16)
        .reshape(seq_rows, head_count, head_size)
    )

    def block_scores(block_start):
        query_index = block_start + jnp.arange(block_rows, dtype=jnp.int32)
        same_clip = segments[:, None] == segments[None, :]
        usable = is_live[None, :] | (query_index[:, None] == key_index[None, :])
        raw_scores = (
            jnp.einsum("qhd,khd->hqk", queries, key_rows, preferred_element_type=jnp.float32)
            * score_scale
        )
        return jnp.where((same_clip & usable)[None], raw_scores, masked_value)

    block_start = 0
    scores = block_scores(block_start)
    row_max = jnp.max(scores, axis=-1, keepdims=True)
    powered = jnp.exp(scores - row_max)
    denominator = jnp.sum(powered, axis=-1, keepdims=True)
    probs_low = (powered / denominator).astype(jnp.bfloat16)
    context_parts = jnp.einsum(
        "hqk,khd->qhd", probs_low, value_rows, preferred_element_type=jnp.float32
    )
    lse_parts = [row_max + jnp.log(denominator)]
    context = context_parts.reshape(seq_rows, model_width).astype(jnp.bfloat16)
    middle = inputs + row_matmul(context, w_out) + out_bias.astype(jnp.float32)
    normed_two, norm_two_back = jax.vjp(
        normalize, middle, ln2_gain.astype(jnp.float32), ln2_bias.astype(jnp.float32)
    )
    act_two = normed_two.astype(jnp.bfloat16)
    hidden_pre = row_matmul(act_two, w_up) + up_bias.astype(jnp.float32)
    hidden_act, gelu_back = jax.vjp(exact_gelu, hidden_pre)
    hidden_low = hidden_act.astype(jnp.bfloat16)
    result = middle + row_matmul(hidden_low, w_down) + down_bias.astype(jnp.float32)
    normed_three, norm_three_back = jax.vjp(
        normalize, result, ln3_gain.astype(jnp.float32), ln3_bias.astype(jnp.float32)
    )
    act_three = normed_three.astype(jnp.bfloat16)
    aligned = row_matmul(act_three, w_align) + align_bias.astype(jnp.float32)
    grad_aligned = recv_align.reshape(seq_rows, align_width)
    grad_w_align = left_transposed(act_three, grad_aligned)
    grad_align_bias = column_sum(grad_aligned)
    grad_result_part, grad_ln3_gain, grad_ln3_bias = norm_three_back(
        right_transposed(grad_aligned, w_align)
    )
    grad_result = recv_grad.reshape(seq_rows, model_width).astype(jnp.float32) + grad_result_part
    grad_mlp = grad_result.astype(jnp.bfloat16)
    grad_w_down = left_transposed(hidden_low, grad_mlp)
    grad_down_bias = column_sum(grad_mlp)
    (grad_pre,) = gelu_back(right_transposed(grad_mlp, w_down))
    grad_pre_low = grad_pre.astype(jnp.bfloat16)
    grad_w_up = left_transposed(act_two, grad_pre_low)
    grad_up_bias = column_sum(grad_pre_low)
    grad_middle_part, grad_ln2_gain, grad_ln2_bias = norm_two_back(
        right_transposed(grad_pre_low, w_up)
    )
    grad_middle = grad_result + grad_middle_part
    grad_branch = grad_middle.astype(jnp.bfloat16)
    grad_w_out = left_transposed(context, grad_branch)
    grad_out_bias = column_sum(grad_branch)
    grad_context = (
        right_transposed(grad_branch, w_out)
        .astype(jnp.bfloat16)
        .reshape(seq_rows, head_count, head_size)
    )
    grad_keys = jnp.zeros((seq_rows, head_count, head_size), jnp.float32)
    grad_values = jnp.zeros((seq_rows, head_count, head_size), jnp.float32)
    query_parts = []
    for block_number, block_start in enumerate(range(0, seq_rows, block_rows)):
        scores = block_scores(block_start)
        probs = jnp.exp(scores - lse_parts[block_number])
        probs_low = probs.astype(jnp.bfloat16)
        grad_values = jnp.einsum(
            "hqk,qhd->khd", probs_low, grad_context, preferred_element_type=jnp.float32
        )
        grad_probs = jnp.einsum(
            "qhd,khd->hqk", grad_context, value_rows, preferred_element_type=jnp.float32
        )
        inner_sum = jnp.sum(grad_probs * probs, axis=-1, keepdims=True)
        grad_scores = (probs * (grad_probs - inner_sum)).astype(jnp.bfloat16)
        query_parts.append(
            jnp.einsum("hqk,khd->qhd", grad_scores, key_rows, preferred_element_type=jnp.float32)
            * score_scale
        )
        grad_keys = (
            jnp.einsum("hqk,qhd->khd", grad_scores, queries, preferred_element_type=jnp.float32)
            * score_scale
        )
    grad_queries = query_parts[0]
    grad_joined = jnp.concatenate(
        [
            grad_queries.reshape(seq_rows, model_width),
            grad_keys.reshape(seq_rows, model_width),
            grad_values.reshape(seq_rows, model_width),
        ],
        axis=1,
    ).astype(jnp.bfloat16)
    grad_w_qkv = left_transposed(act_one, grad_joined)
    grad_q_bias = column_sum(grad_joined[:, :model_width])
    grad_v_bias = column_sum(grad_joined[:, 2 * model_width :])
    grad_input_part, grad_ln1_gain, grad_ln1_bias = norm_one_back(
        right_transposed(grad_joined, w_qkv)
    )
    grad_input = grad_middle + grad_input_part

    def block_view(rows):
        return rows.reshape((peer_count, capacity) + rows.shape[1:])

    back_result, back_aligned, back_grad = (
        lax.all_to_all(
            block_view(result.astype(jnp.bfloat16)),
            "batch",
            split_axis=0,
            concat_axis=0,
            tiled=True,
        ),
        lax.all_to_all(
            block_view(aligned.astype(jnp.bfloat16)),
            "batch",
            split_axis=0,
            concat_axis=0,
            tiled=True,
        ),
        lax.all_to_all(
            block_view(grad_input.astype(jnp.bfloat16)),
            "batch",
            split_axis=0,
            concat_axis=0,
            tiled=True,
        ),
    )
    out_tokens = back_result.reshape(seq_rows, model_width)[slot_index]
    aligned_tokens = back_aligned.reshape(seq_rows, align_width)[slot_index]
    grad_tokens = back_grad.reshape(seq_rows, model_width)[slot_index]
    (
        sum_ln1_gain,
        sum_ln1_bias,
        sum_q_bias,
        sum_v_bias,
        sum_out_bias,
        sum_ln2_gain,
        sum_ln2_bias,
        sum_up_bias,
        sum_down_bias,
        sum_ln3_gain,
        sum_ln3_bias,
        sum_align_bias,
    ) = lax.psum(
        (
            grad_ln1_gain,
            grad_ln1_bias,
            grad_q_bias,
            grad_v_bias,
            grad_out_bias,
            grad_ln2_gain,
            grad_ln2_bias,
            grad_up_bias,
            grad_down_bias,
            grad_ln3_gain,
            grad_ln3_bias,
            grad_align_bias,
        ),
        ("batch", "grp"),
    )
    block_sums = (
        lax.psum_scatter(
            tiled_blocks(grad_w_qkv, peer_count, group_count),
            ("batch", "grp"),
            scatter_dimension=0,
            tiled=True,
        ),
        lax.psum_scatter(
            tiled_blocks(grad_w_out, peer_count, group_count),
            ("batch", "grp"),
            scatter_dimension=0,
            tiled=True,
        ),
        lax.psum_scatter(
            tiled_blocks(grad_w_up, peer_count, group_count),
            ("batch", "grp"),
            scatter_dimension=0,
            tiled=True,
        ),
        lax.psum_scatter(
            tiled_blocks(grad_w_down, peer_count, group_count),
            ("batch", "grp"),
            scatter_dimension=0,
            tiled=True,
        ),
        lax.psum_scatter(
            tiled_blocks(grad_w_align, peer_count, group_count),
            ("batch", "grp"),
            scatter_dimension=0,
            tiled=True,
        ),
    )
    sum_w_qkv = block_sums[0][0]
    sum_w_out = block_sums[1][0]
    sum_w_up = block_sums[2][0]
    sum_w_down = block_sums[3][0]
    sum_w_align = block_sums[4][0]
    return (
        out_tokens,
        aligned_tokens,
        grad_tokens,
        sum_ln1_gain,
        sum_ln1_bias,
        sum_w_qkv,
        sum_q_bias,
        sum_v_bias,
        sum_w_out,
        sum_out_bias,
        sum_ln2_gain,
        sum_ln2_bias,
        sum_w_up,
        sum_up_bias,
        sum_w_down,
        sum_down_bias,
        sum_ln3_gain,
        sum_ln3_bias,
        sum_w_align,
        sum_align_bias,
    )


def solution(mesh):
    return jax.shard_map(
        per_device,
        mesh=mesh,
        in_specs=(
            P(("batch", "grp"), None),
            P(("batch", "grp"), None),
            P(("batch", "grp"), None),
            P(("batch", "grp"), None),
            P(("batch", "grp"), None),
            P(),
            P(),
            P(),
            P(),
            P(),
            P(),
            P(),
            P(),
            P(),
            P(),
            P(),
            P(),
            P(),
            P(),
            P(),
            P(),
            P(),
        ),
        out_specs=(
            P(("batch", "grp"), None),
            P(("batch", "grp"), None),
            P(("batch", "grp"), None),
            P(),
            P(),
            P("batch", "grp"),
            P(),
            P(),
            P("batch", "grp"),
            P(),
            P(),
            P(),
            P("batch", "grp"),
            P(),
            P("batch", "grp"),
            P(),
            P(),
            P(),
            P("batch", "grp"),
            P(),
        ),
        check_vma=False,
    )
```

profile of v0, /device:TPU:0, one launch (start us, length us, event | category | flops | bytes accessed | tf_op | source)
XLA Modules:
  0.0 800.7 jit_solution(46928050250351384)
XLA Ops:
  14.4 7.3 all-to-all-start.1
  28.1 4.2 all-to-all-start
  54.3 6.3 all-to-all-start.5
  80.0 3.7 fusion
  84.7 4.9 fusion.30
  92.4 20.0 %multiply_convert_fusion.1 = (bf16[512,3072]{1,0:T(8,128)(2,1)S(1)}, f32[512,3072]{1,0:T(8,128)}, f32[512,3072]{1,0:T(8,128)}) fusion(f32[3072]{0:T(1024)S(1)} %copy-done.41, bf16[768,3072]{1,0:T(8,128)(2,1)} %param.36, f32[512,768]{1,0:T(8,128)S(1)} %get-tuple-element.63, f32[768]{0:T(1024)S(1)} %copy-done.50, f32[768]{0:T(1024)S(1)} %copy-done.37, ...), kind=kOutput, calls=%fused_computation.21 | convolution fusion | flops 2521694208 | bytes 22042624 | tf_op jit(solution)/shard_map/dot_general | solution.py:23
  116.6 6.0 all-to-all-start.4
  122.7 4.2 multiply_reduce_fusion.1
  129.4 11.3 %all-to-all-done.4 = bf16[8,64,768]{2,1,0:T(8,128)(2,1)} async-done(((bf16[8,64,768]{2,1,0:T(8,128)(2,1)}), bf16[8,64,768]{2,1,0:T(8,128)(2,1)}, u32[]{:S(2)}, u32[]{:S(2)}) %all-to-all-start.4) | async-done | bytes 786464 | tf_op jit(solution)/shard_map/all_to_all | solution.py:101
  143.2 9.8 %convert_reduce_fusion = (f32[3072]{0:T(1024)}, bf16[512,3072]{1,0:T(8,128)(2,1)S(1)}) fusion(f32[512,3072]{1,0:T(8,128)} %get-tuple-element.53, f32[512,3072]{1,0:T(8,128)} %get-tuple-element.64, f32[3072]{0:T(1024)S(1)} %copy-done.42, bf16[512,768]{1,0:T(8,128)(2,1)S(1)} %get-tuple-element.45, bf16[3072,768]{1,0:T(8,128)(2,1)} %param.38), kind=kOutput, calls=%fused_computation.18 | convolution fusion | flops 2442654720 | bytes 21258240 | tf_op jit(solution)/shard_map/dot_general | solution.py:33
  153.0 7.0 multiply_reduce_fusion.2
  166.8 4.0 fusion.66
  185.1 4.1 fusion.68
  189.6 13.7 %multiply_reduce_fusion = (f32[12,512]{1,0:T(8,128)S(1)}, f32[12,512,512]{1,2,0:T(8,128)}) fusion(f32[12,512]{1,0:T(8,128)} %log_add_fusion, f32[12,512,512]{1,2,0:T(8,128)} %copy-done.1, pred[512,512]{0,1:T(8,128)(4,1)} %fusion.32, bf16[512,12,64]{0,2,1:T(8,128)(2,1)} %bitcast.196, bf16[512,12,64]{0,2,1:T(8,128)(2,1)} %bitcast.195), kind=kOutput, calls=%fused_computation.8 | convolution fusion | flops 418375680 | bytes 27049984 | tf_op jit(solution)/shard_map/qhd,khd->hqk/dot_general | solution.py:201
  203.4 7.2 multiply_convert_fusion
  219.3 4.4 fusion.65
  224.4 8.9 %fusion.53 = f32[768,3072]{1,0:T(8,128)} fusion(bf16[512,3072]{1,0:T(8,128)(2,1)} %copy-done.55, f32[512,768]{1,0:T(8,128)} %copy-done.9, f32[768]{0:T(1024)} %convert_element_type.155, f32[768]{0:T(1024)S(1)} %copy-done.39, f32[512]{0:T(512)S(1)} %copy-done.48, f32[512]{0:T(512)S(1)} %broadcast_multiply_fusion.2), kind=kOutput, calls=%fused_computation.129 | convolution fusion | flops 2417885184 | bytes 14166016 | tf_op jit(solution)/shard_map/dot_general | solution.py:27
  233.2 12.5 %reshape.372 = f32[8,96,4,768]{3,2,1,0:T(4,128)} reshape(f32[768,3072]{1,0:T(8,128)} %fusion.53) | data formatting | bytes 18874368 | tf_op jit(solution)/shard_map/reshape | solution.py:44
  245.8 9.0 %copy.99 = f32[8,4,96,768]{3,2,1,0:T(8,128)} copy(f32[8,4,96,768]{3,1,2,0:T(4,128)} %bitcast.179) | data formatting | bytes 18874368 | tf_op jit(solution)/shard_map/transpose | solution.py:47
  255.3 8.4 %fusion.67 = f32[3072,768]{0,1:T(8,128)} fusion(bf16[512,3072]{1,0:T(8,128)(2,1)} %copy-done.54, bf16[512,768]{1,0:T(8,128)(2,1)} %copy-done.18), kind=kOutput, calls=%fused_computation.141 | convolution fusion | flops 2415919104 | bytes 13369344 | tf_op jit(solution)/shard_map/dot_general | solution.py:27
  263.7 5.9 copy.112
  269.6 5.4 copy.101
  278.7 28.1 %all_to_all.40 = bf16[8,64,1024]{2,1,0:T(8,128)(2,1)} all-to-all(bf16[8,64,1024]{2,1,0:T(8,128)(2,1)S(1)} %bitcast.210), channel_id=1, replica_groups=mesh['batch'=8,'grp'=4] {'batch'}, dimensions={0} | all-to-all | bytes 2097152 | tf_op jit(solution)/shard_map/all_to_all | solution.py:242
  306.8 4.2 all-to-all-start.2
  311.1 4.8 fusion.57
  320.5 12.9 %all-to-all-done.2 = bf16[8,64,768]{2,1,0:T(8,128)(2,1)} async-done(((bf16[8,64,768]{2,1,0:T(8,128)(2,1)}), bf16[8,64,768]{2,1,0:T(8,128)(2,1)}, u32[]{:S(2)}, u32[]{:S(2)}) %all-to-all-start.2) | async-done | bytes 786464 | tf_op jit(solution)/shard_map/all_to_all | solution.py:235
  333.4 4.4 all-to-all-start.6
  342.7 43.1 %all-reduce = (f32[768]{0:T(1024)}, f32[768]{0:T(1024)}, f32[768]{0:T(1024)}, f32[768]{0:T(1024)}, f32[768]{0:T(1024)}, /*index=5*/f32[768]{0:T(1024)}, f32[768]...) all-reduce(f32[768]{0:T(1024)S(1)} %get-tuple-element.24, ...), channel_id=1, replica_groups=mesh['batch'=8,'grp'=4] {'batch','grp'}, use_global_device_ids=true, to_apply=%region_23.24 | all-reduce | flops 11776 | bytes 94208 | tf_op jit(solution)/shard_map/psum | solution.py:273
  385.8 3.9 gather_fusion.1
  396.5 114.2 %reduce-scatter.6.cloned.1.call-done = f32[1,96,576]{2,1,0:T(8,128)} async-done(((f32[32,96,576]{2,1,0:T(8,128)}), f32[1,96,576]{2,1,0:T(8,128)}) %reduce-scatter.6.cloned.1.call-update) | async-done | bytes 221200 | tf_op jit(solution)/shard_map/reduce_scatter | solution.py:291
  510.7 142.3 %reduce-scatter.10.cloned.1.call-done = f32[1,96,768]{2,1,0:T(8,128)} async-done(((f32[32,96,768]{2,1,0:T(8,128)}), f32[1,96,768]{2,1,0:T(8,128)}) %reduce-scatter.10.cloned.1.call-update) | async-done | bytes 294928 | tf_op jit(solution)/shard_map/reduce_scatter | solution.py:303
  653.0 141.0 %reduce-scatter.12.cloned.1.call-done = f32[1,384,192]{1,2,0:T(8,128)} async-done(((f32[32,384,192]{1,2,0:T(8,128)}), f32[1,384,192]{1,2,0:T(8,128)}) %reduce-scatter.12.cloned.1.call-update) | async-done | bytes 294928 | tf_op jit(solution)/shard_map/reduce_scatter | solution.py:309
  (220 shorter events, 118.9 us)
Async XLA Ops:
  7.2 57.8 %copy-start = (bf16[768,2304]{1,0:T(8,128)(2,1)S(1)}, bf16[768,2304]{1,0:T(8,128)(2,1)}, u32[]{:S(2)}) copy-start(bf16[768,2304]{1,0:T(8,128)(2,1)} %param.29) | copy-start | bytes 10616836
  8.6 44.7 %copy-start.43 = (s32[1,512]{1,0:T(1,128)S(1)}, s32[1,512]{1,0:T(1,128)}, u32[]{:S(2)}) copy-start(s32[1,512]{1,0:T(1,128)} %param.24) | copy-start | bytes 6148
  11.6 42.7 %copy-start.49 = (s32[256,1]{0,1:T(1,128)}, s32[256,1]{0,1:T(1,128)S(1)}, u32[]{:S(2)}) copy-start(s32[256,1]{0,1:T(1,128)S(1)} %compare_select_fusion) | copy-start | bytes 3076
  14.4 13.7 %all-to-all-start.1 = ((bf16[8,1,64]{2,1,0:T(2,128)(2,1)}), bf16[8,1,64]{2,1,0:T(2,128)(2,1)S(1)}, u32[]{:S(2)}, u32[]{:S(2)}) async-start(bf16[8,1,64]{2,1,0:T(2,128)(2,1)} %all_to_all.32), calls=%async_computation.1 | async-start | bytes 8192 | tf_op jit(solution)/shard_map/all_to_all | solution.py:103
  28.1 26.2 %all-to-all-start = ((bf16[8,64,768]{2,1,0:T(8,128)(2,1)}), bf16[8,64,768]{2,1,0:T(8,128)(2,1)}, u32[]{:S(2)}, u32[]{:S(2)}) async-start(bf16[8,64,768]{2,1,0:T(8,128)(2,1)} %bitcast.206), calls=%async_computation | async-start | bytes 1572864 | tf_op jit(solution)/shard_map/all_to_all | solution.py:100
  33.0 32.0 %copy-start.22 = (f32[768]{0:T(1024)}, f32[768]{0:T(1024)S(1)}, u32[]{:S(2)}) copy-start(f32[768]{0:T(1024)S(1)} %convert_element_type.142) | copy-start | bytes 9220
  54.3 62.3 %all-to-all-start.5 = ((bf16[8,64,1024]{2,1,0:T(8,128)(2,1)}), bf16[8,64,1024]{2,1,0:T(8,128)(2,1)}, u32[]{:S(2)}, u32[]{:S(2)}) async-start(bf16[8,64,1024]{2,1,0:T(8,128)(2,1)} %bitcast.193), calls=%async_computation.5 | async-start | bytes 2097152 | tf_op jit(solution)/shard_map/all_to_all | solution.py:102
  89.7 22.7 %slice-start.3 = ((s8[4718592]{0:T(1024)(128)(4,1)}), s8[4194304]{0:T(1024)(128)(4,1)S(1)}, s32[]{:S(2)}) async-start(s8[4718592]{0:T(1024)(128)(4,1)} %bitcast.223), calls=%async_computation.20 | async-start | bytes 8388608
  92.0 20.4 %copy-start.9 = (f32[512,768]{1,0:T(8,128)}, f32[512,768]{1,0:T(8,128)S(1)}, u32[]{:S(2)}) copy-start(f32[512,768]{1,0:T(8,128)S(1)} %get-tuple-element.63) | copy-start | bytes 4718596
  92.4 20.0 %copy-start.46 = (f32[512]{0:T(512)}, f32[512]{0:T(512)S(1)}, u32[]{:S(2)}) copy-start(f32[512]{0:T(512)S(1)} %fusion.43) | copy-start | bytes 6148
  92.4 20.0 %copy-start.51 = (f32[768]{0:T(1024)S(1)}, f32[768]{0:T(1024)}, u32[]{:S(2)}) copy-start(f32[768]{0:T(1024)} %convert_element_type.159) | copy-start | bytes 9220
  92.4 20.0 %slice-start.4 = ((s8[4718592]{0:T(1024)(128)(4,1)}), s8[524288]{0:T(1024)(128)(4,1)S(1)}, s32[]{:S(2)}) async-start(s8[4718592]{0:T(1024)(128)(4,1)} %bitcast.223), calls=%async_computation.21 | async-start | bytes 1048576
  116.6 24.1 %all-to-all-start.4 = ((bf16[8,64,768]{2,1,0:T(8,128)(2,1)}), bf16[8,64,768]{2,1,0:T(8,128)(2,1)}, u32[]{:S(2)}, u32[]{:S(2)}) async-start(bf16[8,64,768]{2,1,0:T(8,128)(2,1)} %bitcast.205), calls=%async_computation.4 | async-start | bytes 1572864 | tf_op jit(solution)/shard_map/all_to_all | solution.py:101
  122.6 273.9 %reduce-scatter.8.cloned.1.call-start = ((), (), s32[]{:S(2)}) async-start(), calls=%async_computation.13 | async-start | bytes 3244032 | tf_op jit(solution)/shard_map/reduce_scatter | solution.py:297
  143.2 9.8 %copy-start.18 = (bf16[512,768]{1,0:T(8,128)(2,1)}, bf16[512,768]{1,0:T(8,128)(2,1)S(1)}, u32[]{:S(2)}) copy-start(bf16[512,768]{1,0:T(8,128)(2,1)S(1)} %get-tuple-element.45) | copy-start | bytes 2359300
  143.2 9.8 %copy-start.10 = (f32[512,768]{1,0:T(8,128)S(1)}, f32[512,768]{1,0:T(8,128)}, u32[]{:S(2)}) copy-start(f32[512,768]{1,0:T(8,128)} %copy-done.9) | copy-start | bytes 4718596
  143.2 9.8 %copy-start.38 = (f32[768]{0:T(1024)S(1)}, f32[768]{0:T(1024)}, u32[]{:S(2)}) copy-start(f32[768]{0:T(1024)} %convert_element_type.154) | copy-start | bytes 9220
  143.2 9.8 %copy-start.47 = (f32[512]{0:T(512)S(1)}, f32[512]{0:T(512)}, u32[]{:S(2)}) copy-start(f32[512]{0:T(512)} %copy-done.46) | copy-start | bytes 6148
  170.8 225.7 %reduce-scatter.14.cloned.1.call-start = ((), (), s32[]{:S(2)}) async-start(), calls=%async_computation.16 | async-start | bytes 3244032 | tf_op jit(solution)/shard_map/reduce_scatter | solution.py:315
  189.3 321.5 %reduce-scatter.6.cloned.1.call-start = ((), (), s32[]{:S(2)}) async-start(), calls=%async_computation.12 | async-start | bytes 8110080 | tf_op jit(solution)/shard_map/reduce_scatter | solution.py:291
  189.5 13.8 %slice-start = ((s8[12582912]{0:T(1024)(128)(4,1)}), s8[4194304]{0:T(1024)(128)(4,1)S(1)}, s32[]{:S(2)}) async-start(s8[12582912]{0:T(1024)(128)(4,1)} %bitcast.175), calls=%async_computation.17 | async-start | bytes 8388608
  189.5 13.8 %slice-start.1 = ((s8[12582912]{0:T(1024)(128)(4,1)}), s8[4194304]{0:T(1024)(128)(4,1)S(1)}, s32[]{:S(2)}) async-start(s8[12582912]{0:T(1024)(128)(4,1)} %bitcast.175), calls=%async_computation.18 | async-start | bytes 8388608
  189.5 13.8 %slice-start.2 = ((s8[12582912]{0:T(1024)(128)(4,1)}), s8[4194304]{0:T(1024)(128)(4,1)S(1)}, s32[]{:S(2)}) async-start(s8[12582912]{0:T(1024)(128)(4,1)} %bitcast.175), calls=%async_computation.19 | async-start | bytes 8388608
  189.5 13.8 %copy-start.6 = (pred[512,512]{0,1:T(8,128)(4,1)S(1)}, pred[512,512]{0,1:T(8,128)(4,1)}, u32[]{:S(2)}) copy-start(pred[512,512]{0,1:T(8,128)(4,1)} %fusion.32) | copy-start | bytes 786436
  189.6 13.8 %copy-start.20 = (f32[12,512]{1,0:T(8,128)S(1)}, f32[12,512]{1,0:T(8,128)}, u32[]{:S(2)}) copy-start(f32[12,512]{1,0:T(8,128)} %log_add_fusion) | copy-start | bytes 73732
  223.7 429.3 %reduce-scatter.10.cloned.1.call-start = ((), (), s32[]{:S(2)}) async-start(), calls=%async_computation.14 | async-start | bytes 9732096 | tf_op jit(solution)/shard_map/reduce_scatter | solution.py:303
  254.8 539.1 %reduce-scatter.12.cloned.1.call-start = ((), (), s32[]{:S(2)}) async-start(), calls=%async_computation.15 | async-start | bytes 9732096 | tf_op jit(solution)/shard_map/reduce_scatter | solution.py:309
  278.6 32.4 %copy-start.23 = (f32[768]{0:T(1024)S(1)}, f32[768]{0:T(1024)}, u32[]{:S(2)}) copy-start(f32[768]{0:T(1024)} %copy-done.22) | copy-start | bytes 9220
  278.6 32.4 %copy-start.25 = (f32[512]{0:T(512)S(1)}, f32[512]{0:T(512)}, u32[]{:S(2)}) copy-start(f32[512]{0:T(512)} %copy-done.24) | copy-start | bytes 6148
  306.8 26.6 %all-to-all-start.2 = ((bf16[8,64,768]{2,1,0:T(8,128)(2,1)}), bf16[8,64,768]{2,1,0:T(8,128)(2,1)}, u32[]{:S(2)}, u32[]{:S(2)}) async-start(bf16[8,64,768]{2,1,0:T(8,128)(2,1)} %bitcast.198), calls=%async_computation.2 | async-start | bytes 1572864 | tf_op jit(solution)/shard_map/all_to_all | solution.py:235
  320.5 22.2 %copy-start.30 = (f32[768]{0:T(1024)S(1)}, f32[768]{0:T(1024)}, u32[]{:S(2)}) copy-start(f32[768]{0:T(1024)} %get-tuple-element.44) | copy-start | bytes 9220
  333.4 59.7 %all-to-all-start.6 = ((bf16[8,64,768]{2,1,0:T(8,128)(2,1)}), bf16[8,64,768]{2,1,0:T(8,128)(2,1)}, u32[]{:S(2)}, u32[]{:S(2)}) async-start(bf16[8,64,768]{2,1,0:T(8,128)(2,1)} %bitcast.201), calls=%async_computation.6 | async-start | bytes 1572864 | tf_op jit(solution)/shard_map/all_to_all | solution.py:249
  (40 other events, 135.5 us)
Sparse Core Ops, SparseCore 0:
  171.0 100.4 reduce-scatter.7
  277.5 105.4 reduce-scatter.13
  389.2 121.4 reduce-scatter.5
  518.0 134.8 reduce-scatter.9
  659.3 134.6 reduce-scatter.11
where the time goes:
time: 809 us; the launch traced here: 801 us
  waiting for transfers between devices  425 us (53%)
  matrix products  118 us (15%)
  local copies, waits for them, and re-layouts  81.8 us (10%)
  blocking collectives  71.2 us (9%)
  other arithmetic  56.2 us (7%)
  starting transfers between devices  33.2 us (4%)
  between operations  14.8 us (2%)
    reduce_scatter x1, waiting for transfers between devices, per_device(): lax.psum_scatter(tiled_blocks(grad_w_up, peer_count, group_count), ('batc...  142 us
    reduce_scatter x1, waiting for transfers between devices, per_device(): lax.psum_scatter(tiled_blocks(grad_w_down, peer_count, group_count), ('ba...  141 us
    reduce_scatter x1, waiting for transfers between devices, per_device(): lax.psum_scatter(tiled_blocks(grad_w_qkv, peer_count, group_count), ('bat...  114 us
    psum x1, blocking collectives, per_device(): lax.psum((grad_ln1_gain, grad_ln1_bias, grad_q_bias, grad_v_bias, grad_ou...  43.1 us
    dot_general x5, matrix products, row_matmul(): return jnp.dot(left_side, right_side, preferred_element_type=jnp.float32)  30 us
    dot_general x5, matrix products, left_transposed(): lax.dot_general(left_side, right_side, (((0,), (0,)), ((), ())), preferre...  29.8 us
    dot_general x5, matrix products, right_transposed(): lax.dot_general(left_side, right_side, (((1,), (1,)), ((), ())), preferre...  29.4 us
    all_to_all x1, blocking collectives, per_device(): lax.all_to_all(block_view(aligned.astype(jnp.bfloat16)), 'batch', split_a...  28.1 us
  transfers between devices with their start and end apart: 11, of which 6 were waited for; matrix products, arithmetic and copies ran while one was open for 27% of the time, Pallas kernels for 0%

commit v1 on v0

--- a/solution.py
+++ b/solution.py
@@ -6,6 +6,29 @@
 H = 12
 layer_eps = 1e-06
 masked_value = -1e30
+
+
+def cut_along(x, dim, peers):
+    before, after = (x.shape[:dim], x.shape[dim + 1 :])
+    return jnp.moveaxis(x.reshape(*before, peers, -1, *after), dim, 0)
+
+
+def laid_out(blocks, dim):
+    lengths = list(blocks.shape[1:])
+    lengths[dim] *= blocks.shape[0]
+    return jnp.moveaxis(blocks, 0, dim).reshape(lengths)
+
+
+def sent_to_each(shard, axis, split_dim, concat_dim):
+    peers, place = (lax.axis_size(axis), lax.axis_index(axis))
+    blocks = cut_along(shard, split_dim, peers)
+    whole = blocks
+    for step in range(1, peers):
+        target, source = ((place + step) % peers, (place - step) % peers)
+        sent = lax.dynamic_index_in_dim(blocks, target, 0)
+        other = lax.ppermute(sent, axis, [(i, (i + step) % peers) for i in range(peers)])
+        whole = lax.dynamic_update_slice_in_dim(whole, other, source, axis=0)
+    return laid_out(whole, concat_dim)
 
 
 def normalize(values, gain_row, shift_row):
@@ -98,7 +121,7 @@
     flag_rows = jnp.ones((tokens.shape[0],), jnp.bfloat16)
     recv_rows, recv_grad, recv_align, recv_flag = (
         lax.all_to_all(pack_rows(tokens), "batch", split_axis=0, concat_axis=0, tiled=True),
-        lax.all_to_all(pack_rows(cot_out), "batch", split_axis=0, concat_axis=0, tiled=True),
+        sent_to_each(pack_rows(cot_out), "batch", 0, 0),
         lax.all_to_all(pack_rows(cot_align), "batch", split_axis=0, concat_axis=0, tiled=True),
         lax.all_to_all(pack_rows(flag_rows), "batch", split_axis=0, concat_axis=0, tiled=True),
     )

time: 809 us -> 813 us (level)
    all_to_all x1 -> x0, waiting for transfers between devices: 11.3 us -> none  [per_device(): lax.all_to_all(pack_rows(cot_out), 'batch', split_axis=0, concat_axis=0,...]
    ppermute x0 -> x7, starting transfers between devices: none -> 10.7 us  [sent_to_each(): lax.ppermute(sent, axis, [(i, (i + step) % peers) for i in range(peers)])]
    ppermute x0 -> x7, waiting for transfers between devices: none -> 9.16 us  [sent_to_each(): lax.ppermute(sent, axis, [(i, (i + step) % peers) for i in range(peers)])]
  transfers between devices with their start and end apart: 11 -> 17, of which waited for: 6 -> 6; matrix products, arithmetic and copies ran while one was open for 27% -> 27% of each run, Pallas kernels for 0% -> 0%
where the time goes in v1:
time: 813 us; the launch traced here: 804 us
  waiting for transfers between devices  419 us (52%)
  matrix products  117 us (14%)
  local copies, waits for them, and re-layouts  88.2 us (11%)
  blocking collectives  76.1 us (9%)
  other arithmetic  53.1 us (7%)
  starting transfers between devices  36.2 us (4%)
  between operations  14.9 us (2%)
    reduce_scatter x1, waiting for transfers between devices, per_device(): lax.psum_scatter(tiled_blocks(grad_w_up, peer_count, group_count), ('batc...  142 us
    reduce_scatter x1, waiting for transfers between devices, per_device(): lax.psum_scatter(tiled_blocks(grad_w_down, peer_count, group_count), ('ba...  141 us
    reduce_scatter x1, waiting for transfers between devices, per_device(): lax.psum_scatter(tiled_blocks(grad_w_qkv, peer_count, group_count), ('bat...  110 us
    psum x1, blocking collectives, per_device(): lax.psum((grad_ln1_gain, grad_ln1_bias, grad_q_bias, grad_v_bias, grad_ou...  44.7 us
    all_to_all x1, blocking collectives, per_device(): lax.all_to_all(block_view(aligned.astype(jnp.bfloat16)), 'batch', split_a...  31.4 us
    dot_general x5, matrix products, left_transposed(): lax.dot_general(left_side, right_side, (((0,), (0,)), ((), ())), preferre...  29.9 us
    dot_general x5, matrix products, row_matmul(): return jnp.dot(left_side, right_side, preferred_element_type=jnp.float32)  29.7 us
    dot_general x5, matrix products, right_transposed(): lax.dot_general(left_side, right_side, (((1,), (1,)), ((), ())), preferre...  27.7 us
  transfers between devices with their start and end apart: 17, of which 6 were waited for; matrix products, arithmetic and copies ran while one was open for 27% of the time, Pallas kernels for 0%

profile of v1, /device:TPU:0, one launch (start us, length us, event | category | flops | bytes accessed | tf_op | source)
XLA Modules:
  0.0 804.2 jit_solution(8827934272651982813)
XLA Ops:
  13.2 7.3 all-to-all-start.1
  26.8 4.2 all-to-all-start
  67.8 9.1 %collective-permute-done.2 = bf16[1,1,64,768]{3,2,0,1:T(8,128)(2,1)S(1)} collective-permute-done((bf16[1,1,64,768]{3,2,0,1:T(8,128)(2,1)S(1)}, bf16[1,1,64,768]{3,2,0,1:T(8,128)(2,1)S(1)}, u32[]{:S(2)}, u32[]{:S(2)}) %collective-permute-start.2) | collective-permute-done | bytes 98336 | tf_op jit(solution)/shard_map/ppermute | solution.py:29
  80.2 4.3 all-to-all-start.4
  104.4 3.7 fusion
  109.1 5.3 fusion.30
  117.3 19.6 %multiply_convert_fusion.1 = (bf16[512,3072]{1,0:T(8,128)(2,1)S(1)}, f32[512,3072]{1,0:T(8,128)}, f32[512,3072]{1,0:T(8,128)}) fusion(f32[3072]{0:T(1024)S(1)} %copy-done.41, bf16[768,3072]{1,0:T(8,128)(2,1)} %param.36, f32[512,768]{1,0:T(8,128)S(1)} %get-tuple-element.70, f32[768]{0:T(1024)S(1)} %copy-done.48, f32[768]{0:T(1024)S(1)} %copy-done.37, ...), kind=kOutput, calls=%fused_computation.21 | convolution fusion | flops 2521694208 | bytes 22042624 | tf_op jit(solution)/shard_map/dot_general | solution.py:46
  141.7 4.3 multiply_reduce_fusion.1
  149.0 9.7 %convert_reduce_fusion = (f32[3072]{0:T(1024)}, bf16[512,3072]{1,0:T(8,128)(2,1)}) fusion(f32[512,3072]{1,0:T(8,128)} %get-tuple-element.53, f32[512,3072]{1,0:T(8,128)} %get-tuple-element.71, f32[3072]{0:T(1024)S(1)} %copy-done.42, bf16[512,768]{1,0:T(8,128)(2,1)S(1)} %get-tuple-element.45, bf16[3072,768]{1,0:T(8,128)(2,1)S(1)} %bitcast.227), kind=kOutput, calls=%fused_computation.18 | convolution fusion | flops 2442654720 | bytes 21258240 | tf_op jit(solution)/shard_map/dot_general | solution.py:56
  158.7 5.5 multiply_reduce_fusion.2
  169.0 4.1 fusion.66
  181.5 3.5 convolution_convert_fusion
  187.3 4.1 fusion.68
  191.8 13.7 %multiply_reduce_fusion = (f32[12,512]{1,0:T(8,128)S(1)}, f32[12,512,512]{1,2,0:T(8,128)}) fusion(f32[12,512]{1,0:T(8,128)} %log_add_fusion, f32[12,512,512]{1,2,0:T(8,128)} %copy-done.1, pred[512,512]{0,1:T(8,128)(4,1)} %fusion.32, bf16[512,12,64]{0,2,1:T(8,128)(2,1)} %bitcast.198, bf16[512,12,64]{0,2,1:T(8,128)(2,1)} %bitcast.197), kind=kOutput, calls=%fused_computation.8 | convolution fusion | flops 418375680 | bytes 27049984 | tf_op jit(solution)/shard_map/qhd,khd->hqk/dot_general | solution.py:224
  205.6 7.2 multiply_convert_fusion
  221.5 4.4 fusion.65
  226.5 8.9 %fusion.53 = f32[768,3072]{1,0:T(8,128)} fusion(bf16[512,3072]{1,0:T(8,128)(2,1)} %get-tuple-element.47, f32[512,768]{1,0:T(8,128)} %copy-done.9, f32[768]{0:T(1024)} %convert_element_type.155, f32[768]{0:T(1024)S(1)} %copy-done.39, f32[512]{0:T(512)} %copy-done.45, f32[512]{0:T(512)S(1)} %broadcast_multiply_fusion.2), kind=kOutput, calls=%fused_computation.143 | convolution fusion | flops 2417885184 | bytes 14166016 | tf_op jit(solution)/shard_map/dot_general | solution.py:50
  235.4 12.5 %reshape.367 = f32[8,96,4,768]{3,2,1,0:T(4,128)} reshape(f32[768,3072]{1,0:T(8,128)} %fusion.53) | data formatting | bytes 18874368 | tf_op jit(solution)/shard_map/reshape | solution.py:67
  247.9 9.0 %copy.99 = f32[8,4,96,768]{3,2,1,0:T(8,128)} copy(f32[8,4,96,768]{3,1,2,0:T(4,128)} %bitcast.179) | data formatting | bytes 18874368 | tf_op jit(solution)/shard_map/transpose | solution.py:70
  257.4 8.4 %fusion.67 = f32[3072,768]{0,1:T(8,128)} fusion(bf16[512,3072]{1,0:T(8,128)(2,1)} %copy-done.52, bf16[512,768]{1,0:T(8,128)(2,1)} %copy-done.18), kind=kOutput, calls=%fused_computation.155 | convolution fusion | flops 2415919104 | bytes 13369344 | tf_op jit(solution)/shard_map/dot_general | solution.py:50
  265.8 5.9 copy.112
  271.7 5.3 copy.101
  280.8 31.4 %all_to_all.35 = bf16[8,64,1024]{2,1,0:T(8,128)(2,1)} all-to-all(bf16[8,64,1024]{2,1,0:T(8,128)(2,1)S(1)} %bitcast.211), channel_id=1, replica_groups=mesh['batch'=8,'grp'=4] {'batch'}, dimensions={0} | all-to-all | bytes 2097152 | tf_op jit(solution)/shard_map/all_to_all | solution.py:265
  312.2 4.2 all-to-all-start.2
  316.5 4.8 fusion.57
  326.6 13.0 %all-to-all-done.2 = bf16[8,64,768]{2,1,0:T(8,128)(2,1)} async-done(((bf16[8,64,768]{2,1,0:T(8,128)(2,1)}), bf16[8,64,768]{2,1,0:T(8,128)(2,1)}, u32[]{:S(2)}, u32[]{:S(2)}) %all-to-all-start.2) | async-done | bytes 786464 | tf_op jit(solution)/shard_map/all_to_all | solution.py:258
  339.6 4.4 all-to-all-start.5
  349.0 44.7 %all-reduce = (f32[768]{0:T(1024)}, f32[768]{0:T(1024)}, f32[768]{0:T(1024)}, f32[768]{0:T(1024)}, f32[768]{0:T(1024)}, /*index=5*/f32[768]{0:T(1024)}, f32[768]...) all-reduce(f32[768]{0:T(1024)S(1)} %get-tuple-element.24, ...), channel_id=1, replica_groups=mesh['batch'=8,'grp'=4] {'batch','grp'}, use_global_device_ids=true, to_apply=%region_23.24 | all-reduce | flops 11776 | bytes 94208 | tf_op jit(solution)/shard_map/psum | solution.py:296
  393.7 3.9 gather_fusion.1
  404.3 110.0 %reduce-scatter.6.cloned.1.call-done = f32[1,96,576]{2,1,0:T(8,128)} async-done(((f32[32,96,576]{2,1,0:T(8,128)}), f32[1,96,576]{2,1,0:T(8,128)}) %reduce-scatter.6.cloned.1.call-update) | async-done | bytes 221200 | tf_op jit(solution)/shard_map/reduce_scatter | solution.py:314
  514.3 142.3 %reduce-scatter.10.cloned.1.call-done = f32[1,96,768]{2,1,0:T(8,128)} async-done(((f32[32,96,768]{2,1,0:T(8,128)}), f32[1,96,768]{2,1,0:T(8,128)}) %reduce-scatter.10.cloned.1.call-update) | async-done | bytes 294928 | tf_op jit(solution)/shard_map/reduce_scatter | solution.py:326
  656.6 141.0 %reduce-scatter.12.cloned.1.call-done = f32[1,384,192]{1,2,0:T(8,128)} async-done(((f32[32,384,192]{1,2,0:T(8,128)}), f32[1,384,192]{1,2,0:T(8,128)}) %reduce-scatter.12.cloned.1.call-update) | async-done | bytes 294928 | tf_op jit(solution)/shard_map/reduce_scatter | solution.py:332
  (244 shorter events, 129.7 us)
Async XLA Ops:
  7.2 82.1 %copy-start = (bf16[768,2304]{1,0:T(8,128)(2,1)S(1)}, bf16[768,2304]{1,0:T(8,128)(2,1)}, u32[]{:S(2)}) copy-start(bf16[768,2304]{1,0:T(8,128)(2,1)} %param.29) | copy-start | bytes 10616836
  10.3 47.0 %copy-start.47 = (s32[256,1]{0,1:T(1,128)}, s32[256,1]{0,1:T(1,128)S(1)}, u32[]{:S(2)}) copy-start(s32[256,1]{0,1:T(1,128)S(1)} %compare_select_fusion) | copy-start | bytes 3076
  13.2 13.7 %all-to-all-start.1 = ((bf16[8,1,64]{2,1,0:T(2,128)(2,1)}), bf16[8,1,64]{2,1,0:T(2,128)(2,1)S(1)}, u32[]{:S(2)}, u32[]{:S(2)}) async-start(bf16[8,1,64]{2,1,0:T(2,128)(2,1)} %all_to_all.28), calls=%async_computation.1 | async-start | bytes 8192 | tf_op jit(solution)/shard_map/all_to_all | solution.py:126
  20.5 38.4 %copy-start.43 = (s32[1,512]{1,0:T(1,128)S(1)}, s32[1,512]{1,0:T(1,128)}, u32[]{:S(2)}) copy-start(s32[1,512]{1,0:T(1,128)} %param.24) | copy-start | bytes 6148
  26.8 53.4 %all-to-all-start = ((bf16[8,64,768]{2,1,0:T(8,128)(2,1)}), bf16[8,64,768]{2,1,0:T(8,128)(2,1)}, u32[]{:S(2)}, u32[]{:S(2)}) async-start(bf16[8,64,768]{2,1,0:T(8,128)(2,1)} %bitcast.206), calls=%async_computation | async-start | bytes 1572864 | tf_op jit(solution)/shard_map/all_to_all | solution.py:123
  35.7 19.8 %collective-permute-start = (bf16[1,1,64,768]{3,2,0,1:T(8,128)(2,1)}, bf16[1,1,64,768]{3,2,0,1:T(8,128)(2,1)}, u32[]{:S(2)}, u32[]{:S(2)}) collective-permute-start(bf16[1,1,64,768]{3,2,0,1:T(8,128)(2,1)} %constant_dynamic-slice_fusion.6), channel_id=1, source_target_pairs={{0,4},{4,8},{8,12},{12,16},{16,20},{20,24},{24,28},{28,0},{1,5},{5... | collective-permute-start | bytes 294920 | tf_op jit(solution)/shard_map/ppermute | solution.py:29
  38.2 49.6 %copy-start.22 = (f32[768]{0:T(1024)}, f32[768]{0:T(1024)S(1)}, u32[]{:S(2)}) copy-start(f32[768]{0:T(1024)S(1)} %convert_element_type.142) | copy-start | bytes 9220
  57.4 9.2 %collective-permute-start.1 = (bf16[1,1,64,768]{3,2,0,1:T(8,128)(2,1)S(1)}, bf16[1,1,64,768]{3,2,0,1:T(8,128)(2,1)S(1)}, u32[]{:S(2)}, u32[]{:S(2)}) collective-permute-start(bf16[1,1,64,768]{3,2,0,1:T(8,128)(2,1)S(1)} %get-tuple-element.65), channel_id=1, source_target_pairs={{0,8},{4,12},{8,16},{12,20},{16,24},{20,28},{24,0},{28,4},{1,9},{5... | collective-permute-start | bytes 294920 | tf_op jit(solution)/shard_map/ppermute | solution.py:29
  59.8 19.7 %collective-permute-start.6 = (bf16[1,1,64,768]{3,2,0,1:T(8,128)(2,1)S(1)}, bf16[1,1,64,768]{3,2,0,1:T(8,128)(2,1)S(1)}, u32[]{:S(2)}, u32[]{:S(2)}) collective-permute-start(bf16[1,1,64,768]{3,2,0,1:T(8,128)(2,1)S(1)} %get-tuple-element.60), channel_id=1, source_target_pairs={{0,28},{4,0},{8,4},{12,8},{16,12},{20,16},{24,20},{28,24},{1,29},{... | collective-permute-start | bytes 294920 | tf_op jit(solution)/shard_map/ppermute | solution.py:29
  63.1 15.8 %collective-permute-start.5 = (bf16[1,1,64,768]{3,2,0,1:T(8,128)(2,1)S(1)}, bf16[1,1,64,768]{3,2,0,1:T(8,128)(2,1)S(1)}, u32[]{:S(2)}, u32[]{:S(2)}) collective-permute-start(bf16[1,1,64,768]{3,2,0,1:T(8,128)(2,1)S(1)} %get-tuple-element.61), channel_id=1, source_target_pairs={{0,24},{4,28},{8,0},{12,4},{16,8},{20,12},{24,16},{28,20},{1,25},{... | collective-permute-start | bytes 294920 | tf_op jit(solution)/shard_map/ppermute | solution.py:29
  63.2 15.0 %collective-permute-start.4 = (bf16[1,1,64,768]{3,2,0,1:T(8,128)(2,1)S(1)}, bf16[1,1,64,768]{3,2,0,1:T(8,128)(2,1)S(1)}, u32[]{:S(2)}, u32[]{:S(2)}) collective-permute-start(bf16[1,1,64,768]{3,2,0,1:T(8,128)(2,1)S(1)} %get-tuple-element.62), channel_id=1, source_target_pairs={{0,20},{4,24},{8,28},{12,0},{16,4},{20,8},{24,12},{28,16},{1,21},{... | collective-permute-start | bytes 294920 | tf_op jit(solution)/shard_map/ppermute | solution.py:29
  64.2 13.4 %collective-permute-start.3 = (bf16[1,1,64,768]{3,2,0,1:T(8,128)(2,1)S(1)}, bf16[1,1,64,768]{3,2,0,1:T(8,128)(2,1)S(1)}, u32[]{:S(2)}, u32[]{:S(2)}) collective-permute-start(bf16[1,1,64,768]{3,2,0,1:T(8,128)(2,1)S(1)} %get-tuple-element.63), channel_id=1, source_target_pairs={{0,16},{4,20},{8,24},{12,28},{16,0},{20,4},{24,8},{28,12},{1,17},{... | collective-permute-start | bytes 294920 | tf_op jit(solution)/shard_map/ppermute | solution.py:29
  66.5 10.4 %collective-permute-start.2 = (bf16[1,1,64,768]{3,2,0,1:T(8,128)(2,1)S(1)}, bf16[1,1,64,768]{3,2,0,1:T(8,128)(2,1)S(1)}, u32[]{:S(2)}, u32[]{:S(2)}) collective-permute-start(bf16[1,1,64,768]{3,2,0,1:T(8,128)(2,1)S(1)} %get-tuple-element.64), channel_id=1, source_target_pairs={{0,12},{4,16},{8,20},{12,24},{16,28},{20,0},{24,4},{28,8},{1,13},{... | collective-permute-start | bytes 294920 | tf_op jit(solution)/shard_map/ppermute | solution.py:29
  80.2 61.5 %all-to-all-start.4 = ((bf16[8,64,1024]{2,1,0:T(8,128)(2,1)}), bf16[8,64,1024]{2,1,0:T(8,128)(2,1)}, u32[]{:S(2)}, u32[]{:S(2)}) async-start(bf16[8,64,1024]{2,1,0:T(8,128)(2,1)} %bitcast.195), calls=%async_computation.4 | async-start | bytes 2097152 | tf_op jit(solution)/shard_map/all_to_all | solution.py:125
  84.5 319.8 %reduce-scatter.8.cloned.1.call-start = ((), (), s32[]{:S(2)}) async-start(), calls=%async_computation.12 | async-start | bytes 3244032 | tf_op jit(solution)/shard_map/reduce_scatter | solution.py:320
  114.5 22.4 %slice-start.3 = ((s8[4718592]{0:T(1024)(128)(4,1)}), s8[4194304]{0:T(1024)(128)(4,1)S(1)}, s32[]{:S(2)}) async-start(s8[4718592]{0:T(1024)(128)(4,1)} %bitcast.224), calls=%async_computation.19 | async-start | bytes 8388608
  116.8 20.0 %copy-start.9 = (f32[512,768]{1,0:T(8,128)}, f32[512,768]{1,0:T(8,128)S(1)}, u32[]{:S(2)}) copy-start(f32[512,768]{1,0:T(8,128)S(1)} %get-tuple-element.70) | copy-start | bytes 4718596
  117.2 19.7 %copy-start.45 = (f32[512]{0:T(512)}, f32[512]{0:T(512)S(1)}, u32[]{:S(2)}) copy-start(f32[512]{0:T(512)S(1)} %fusion.43) | copy-start | bytes 6148
  117.2 19.7 %copy-start.49 = (f32[768]{0:T(1024)S(1)}, f32[768]{0:T(1024)}, u32[]{:S(2)}) copy-start(f32[768]{0:T(1024)} %convert_element_type.159) | copy-start | bytes 9220
  117.2 19.7 %slice-start.4 = ((s8[4718592]{0:T(1024)(128)(4,1)}), s8[524288]{0:T(1024)(128)(4,1)S(1)}, s32[]{:S(2)}) async-start(s8[4718592]{0:T(1024)(128)(4,1)} %bitcast.224), calls=%async_computation.20 | async-start | bytes 1048576
  173.1 231.2 %reduce-scatter.14.cloned.1.call-start = ((), (), s32[]{:S(2)}) async-start(), calls=%async_computation.15 | async-start | bytes 3244032 | tf_op jit(solution)/shard_map/reduce_scatter | solution.py:338
  191.5 322.8 %reduce-scatter.6.cloned.1.call-start = ((), (), s32[]{:S(2)}) async-start(), calls=%async_computation.11 | async-start | bytes 8110080 | tf_op jit(solution)/shard_map/reduce_scatter | solution.py:314
  191.7 13.8 %slice-start = ((s8[12582912]{0:T(1024)(128)(4,1)}), s8[4194304]{0:T(1024)(128)(4,1)S(1)}, s32[]{:S(2)}) async-start(s8[12582912]{0:T(1024)(128)(4,1)} %bitcast.175), calls=%async_computation.16 | async-start | bytes 8388608
  191.7 13.8 %slice-start.1 = ((s8[12582912]{0:T(1024)(128)(4,1)}), s8[4194304]{0:T(1024)(128)(4,1)S(1)}, s32[]{:S(2)}) async-start(s8[12582912]{0:T(1024)(128)(4,1)} %bitcast.175), calls=%async_computation.17 | async-start | bytes 8388608
  191.8 13.8 %slice-start.2 = ((s8[12582912]{0:T(1024)(128)(4,1)}), s8[4194304]{0:T(1024)(128)(4,1)S(1)}, s32[]{:S(2)}) async-start(s8[12582912]{0:T(1024)(128)(4,1)} %bitcast.175), calls=%async_computation.18 | async-start | bytes 8388608
  225.9 430.7 %reduce-scatter.10.cloned.1.call-start = ((), (), s32[]{:S(2)}) async-start(), calls=%async_computation.13 | async-start | bytes 9732096 | tf_op jit(solution)/shard_map/reduce_scatter | solution.py:326
  256.9 540.6 %reduce-scatter.12.cloned.1.call-start = ((), (), s32[]{:S(2)}) async-start(), calls=%async_computation.14 | async-start | bytes 9732096 | tf_op jit(solution)/shard_map/reduce_scatter | solution.py:332
  280.7 35.7 %copy-start.23 = (f32[768]{0:T(1024)S(1)}, f32[768]{0:T(1024)}, u32[]{:S(2)}) copy-start(f32[768]{0:T(1024)} %copy-done.22) | copy-start | bytes 9220
  280.8 35.7 %copy-start.25 = (f32[512]{0:T(512)S(1)}, f32[512]{0:T(512)}, u32[]{:S(2)}) copy-start(f32[512]{0:T(512)} %copy-done.24) | copy-start | bytes 6148
  312.2 27.4 %all-to-all-start.2 = ((bf16[8,64,768]{2,1,0:T(8,128)(2,1)}), bf16[8,64,768]{2,1,0:T(8,128)(2,1)}, u32[]{:S(2)}, u32[]{:S(2)}) async-start(bf16[8,64,768]{2,1,0:T(8,128)(2,1)} %bitcast.200), calls=%async_computation.2 | async-start | bytes 1572864 | tf_op jit(solution)/shard_map/all_to_all | solution.py:258
  326.6 22.4 %copy-start.30 = (f32[768]{0:T(1024)S(1)}, f32[768]{0:T(1024)}, u32[]{:S(2)}) copy-start(f32[768]{0:T(1024)} %get-tuple-element.57) | copy-start | bytes 9220
  339.6 61.3 %all-to-all-start.5 = ((bf16[8,64,768]{2,1,0:T(8,128)(2,1)}), bf16[8,64,768]{2,1,0:T(8,128)(2,1)}, u32[]{:S(2)}, u32[]{:S(2)}) async-start(bf16[8,64,768]{2,1,0:T(8,128)(2,1)} %bitcast.203), calls=%async_computation.5 | async-start | bytes 1572864 | tf_op jit(solution)/shard_map/all_to_all | solution.py:272
  (47 other events, 225.8 us)
Sparse Core Ops, SparseCore 0:
  173.2 102.9 reduce-scatter.7
  282.2 104.4 reduce-scatter.13
  392.9 121.4 reduce-scatter.5
  521.6 134.8 reduce-scatter.9
  662.9 134.5 reduce-scatter.11
